TPU v7x, 32 devices: a whole 2x2x4 slice. The times are simulated.
32 devices in a mesh: str: 8 (over z, x), fac: 4 (over y, core).
Axes of the slice: x: 2, y: 2, z: 4, core: 2. Of those that a mesh axis runs over, the one named last changes fastest.
Arguments:
- amplitudes: bfloat16 [2, 4096, 4096], P(None, 'str'), may hold values from -6 to 6
- beta_index: int32 [2, 32, 12], replicated, may hold values from 0 to 31, all different within a row; in each aligned block of 32 rows (0 to 31, 32 to 63, ..., all dimensions but the last counted through in order) at most 24 rows name the same one
- beta_tile: int32 [2, 12], replicated, may hold values from 0 to 15
- beta_flip: int32 [2, 4096], replicated, may hold values 0 or 1
- alpha_index: int32 [2, 32, 12], replicated, may hold values from 0 to 31, all different within a row; in each aligned block of 32 rows (0 to 31, 32 to 63, ..., all dimensions but the last counted through in order) at most 24 rows name the same one
- alpha_tile: int32 [2, 12], replicated, may hold values from 0 to 15
- alpha_flip: int32 [2, 4096], replicated, may hold values 0 or 1
- beta_tiles: bfloat16 [16, 128, 128], replicated, may hold values from -0.15625 to 0.15625
- alpha_tiles: bfloat16 [16, 128, 128], replicated, may hold values from -0.109375 to 0.109375
Outputs:
- sigma: float32 [2, 4096, 4096], P(None, 'fac', 'str')
Inputs may be any that keep to these rules, and one draw needn't show every extreme that they name: `beta_index`: each block row of one factor's beta operator names 12 different block columns; within one factor's operator no block column is named by more than 24 block rows, and in some factor one column is named by exactly 24. `alpha_index`: each block row of one factor's alpha operator names 12 different block columns; within one factor's operator no block column is named by more than 24 block rows, and in some factor one column is named by exactly 24.
All inputs are finite; a program needn't handle non-finite values.
Results may differ from a plain program's by a relative error of at most 0.012.
Values may be sent and summed in bfloat16 or wider, within the bound.
A program may use at most 128 MiB of HBM per device.

v0:
```python
import functools
import math

import jax
import jax.numpy as jnp
from jax import lax
from jax.experimental import pallas as pl
from jax.experimental.pallas import tpu as pltpu
from jax.sharding import PartitionSpec as P

MESH = pl.DeviceIdType.MESH


def split_position(pos, F):
    factors = F // 2
    return pos % factors, pos // factors


def kernel(dims, amp_hbm, bflip_hbm, aflip_hbm, btab_hbm, atab_hbm, bidx_hbm, aidx_hbm, btile_hbm, atile_hbm, out, *scratch):
    S, F, C, A, T, K, NB, H = dims
    amp, half_send, term_send, pair_recv, wb, wa, bflip, aflip, btab, atab, sign_a, bidx, aidx, btile, atile, raw = scratch[:16]
    recv = scratch[16 : 16 + C]
    a_sem, t_sem, s_send, s_recv, p_send, p_recv, f_send, f_recv = scratch[16 + C :]
    me = lax.axis_index("str")
    pos = lax.axis_index("fac")
    fac, part = split_position(pos, F)
    chips = F // 2
    chip = pos // 2
    core = pos % 2
    per = term_send.shape[1] // F

    barrier = pltpu.get_barrier_semaphore()

    def greet_str(t, _):
        pl.semaphore_signal(barrier, inc=1, device_id={"str": (me + 1 + t) % S}, device_id_type=MESH)
        return 0

    def greet_fac(t, _):
        peer = ((chip + 1 + t) % chips) * 2 + core
        pl.semaphore_signal(barrier, inc=1, device_id={"fac": peer}, device_id_type=MESH)
        return 0

    partner = chip * 2 + 1 - core
    lax.fori_loop(0, S - 1, greet_str, 0)
    lax.fori_loop(0, chips - 1, greet_fac, 0)
    pl.semaphore_signal(barrier, inc=1, device_id={"fac": partner}, device_id_type=MESH)

    tables = [
        pltpu.make_async_copy(src, dst, t_sem.at[n])
        for n, (src, dst) in enumerate(
            [
                (bflip_hbm, bflip),
                (aflip_hbm, aflip),
                (btab_hbm, btab),
                (bidx_hbm, bidx),
                (btile_hbm, btile),
                (atab_hbm, atab),
                (aidx_hbm, aidx),
                (atile_hbm, atile),
            ]
        )
    ]

    strip = A * T // 8

    def load(k):
        return pltpu.make_async_copy(amp_hbm.at[part, pl.ds(k * strip, strip)], raw.at[pl.ds(k * strip, strip)], a_sem.at[k])

    def start_load(k, _):
        load(k).start()
        return 0

    for copy in tables[:5]:
        copy.start()
    lax.fori_loop(0, 8, start_load, 0)
    for copy in tables[5:]:
        copy.start()

    def signs(flips, block):
        value = flips[:, pl.ds(block * T if isinstance(block, int) else pl.multiple_of(block * T, T), T)].astype(jnp.float32)
        mine = lax.broadcasted_iota(jnp.int32, value.shape, 0) == fac
        return 1 - 2 * jnp.sum(jnp.where(mine, value, 0.0), axis=0, keepdims=True)

    tables[1].wait()
    for r in range(A):
        row = signs(aflip, me * A + r)
        sign_a[pl.ds(r * T, T), :] = jnp.broadcast_to(row, (T, T)).T.astype(jnp.bfloat16)
    tables[4].wait()
    tables[2].wait()
    for s in range(K):
        wb[pl.ds(s * T, T), :] = btab[btile[fac, s]].T
    tables[0].wait()
    tables[3].wait()

    def sign(r, _):
        load(r).wait()
        rows = pl.ds(pl.multiple_of(r * strip, strip), strip)
        row_sign = sign_a[rows, :]
        for k in range(NB):
            amp[k, rows, :] = raw[rows, pl.ds(k * T, T)] * signs(bflip, k).astype(jnp.bfloat16) * row_sign
        return 0

    lax.fori_loop(0, 8, sign, 0)
    pl.semaphore_wait(barrier, S - 1 + chips)

    mid = S // 2

    def dest(t):
        side = (me // mid + 1 + t // mid) % 2
        return side * mid + (me + 1 + t) % mid

    def beta(q, c):
        j = q * C + c
        lhs = jnp.concatenate([amp[bidx[s, fac, j]] for s in range(K)], axis=1)
        res = jnp.dot(lhs, wb[...], preferred_element_type=jnp.float32)
        return res.astype(jnp.bfloat16).reshape(A, T, T)

    def str_copy(c, q, src):
        return pltpu.make_async_remote_copy(
            src_ref=half_send.at[c, q],
            dst_ref=recv[c].at[pl.ds(src * A, A)],
            send_sem=s_send.at[c, q],
            recv_sem=s_recv.at[c, src],
            device_id={"str": q},
            device_id_type=MESH,
        )

    for c in range(C):

        def step(t, _):
            q = dest(t)
            half_send[c, q] = beta(q, c)
            str_copy(c, q, me).start()
            return 0

        lax.fori_loop(0, S - 1, step, 0)
        recv[c][pl.ds(me * A, A)] = beta(me, c)

    for copy in tables[5:]:
        copy.wait()
    for s in range(K):
        wa[:, pl.ds(s * T, T)] = atab[atile[fac, s]]

    piece = per // H
    groups = chips * H

    def place(g):
        return (chip + 1 + g // H) % chips, g % H

    def pair_copy(c, y, h, owner):
        return pltpu.make_async_remote_copy(
            src_ref=term_send.at[c, pl.ds((y * 2 + owner) * per + h * piece, piece)],
            dst_ref=pair_recv.at[c, y, h],
            send_sem=p_send.at[c, y, h],
            recv_sem=p_recv.at[c, y, h],
            device_id={"fac": partner},
            device_id_type=MESH,
        )

    def fac_copy(c, y, h, src):
        src_fac, src_part = split_position(src, F)
        return pltpu.make_async_remote_copy(
            src_ref=term_send.at[c, pl.ds((y * 2 + core) * per + h * piece, piece)],
            dst_ref=out.at[src_fac // 2, src_part, pl.ds(h * piece, piece), pl.ds(c * T, T)],
            send_sem=f_send.at[c, y, h],
            recv_sem=f_recv.at[c, src // 2, h],
            device_id={"fac": y * 2 + core},
            device_id_type=MESH,
        )

    def own_copy(c):
        return pltpu.make_async_copy(
            term_send.at[c, pl.ds(pos * per, per)],
            out.at[fac // 2, part, :, pl.ds(c * T, T)],
            f_send.at[c, chip, 0],
        )

    for c in range(C):

        def arrive(t, _):
            src = (me + 1 + t) % S
            str_copy(c, src, src).wait_recv()
            return 0

        lax.fori_loop(0, S - 1, arrive, 0)

        def alpha(i):
            rhs = jnp.concatenate([recv[c][aidx[s, fac, i]] for s in range(K)], axis=0)
            return jnp.dot(wa[...], rhs, preferred_element_type=jnp.float32)

        def store(i, value):
            term_send[c, pl.ds(pl.multiple_of(i * T, T), T), :] = value.astype(jnp.bfloat16)

        def for_partner(g):
            y, h = place(g)

            def block(b, _):
                i = (y * 2 + 1 - core) * (per // T) + h * (piece // T) + b
                store(i, alpha(i))
                return 0

            lax.fori_loop(0, piece // T, block, 0)
            pair_copy(c, y, h, 1 - core).start()

        def for_self(g):
            y, h = place(g)
            pair_copy(c, y, h, core).wait_recv()

            def block(b, _):
                i = (y * 2 + core) * (per // T) + h * (piece // T) + b
                other = pair_recv[c, y, h, pl.ds(pl.multiple_of(b * T, T), T), :]
                store(i, alpha(i) + other.astype(jnp.float32))
                return 0

            lax.fori_loop(0, piece // T, block, 0)

        def away(g, _):
            for_partner(g + 1)
            for_self(g)
            y, h = place(g)
            fac_copy(c, y, h, pos).start()
            return 0

        def home(g, _):
            for_partner(g + 1)
            for_self(g)
            return 0

        for_partner(0)
        lax.fori_loop(0, groups - H, away, 0)
        lax.fori_loop(groups - H, groups - 1, home, 0)
        for_self(groups - 1)
        own_copy(c).start()

    for c in range(C):

        def finish_str(t, _):
            str_copy(c, (me + 1 + t) % S, me).wait_send()
            return 0

        lax.fori_loop(0, S - 1, finish_str, 0)

        def finish_pair(g, _):
            y, h = place(g)
            pair_copy(c, y, h, 1 - core).wait_send()
            return 0

        lax.fori_loop(0, groups, finish_pair, 0)

        def finish_fac(g, _):
            y, h = place(g)
            fac_copy(c, y, h, pos).wait_send()
            fac_copy(c, y, h, y * 2 + core).wait_recv()
            return 0

        lax.fori_loop(0, groups - H, finish_fac, 0)
        own_copy(c).wait()


def local(S, F, amplitudes, beta_index, beta_tile, beta_flip, alpha_index, alpha_tile, alpha_flip, beta_tiles, alpha_tiles):
    NF, NB, K = beta_index.shape
    NT, T, _ = beta_tiles.shape
    parts, height, width = amplitudes.shape
    total = height * S
    A = height // T
    C = width // S // T
    assert F == 2 * NF and parts == 2 and NF % 2 == 0 and height % 128 == 0
    per = total // F
    H = math.gcd(per // T, 4)
    ids = (beta_index.transpose(2, 0, 1), alpha_index.transpose(2, 0, 1), beta_tile, alpha_tile)
    hbm = pl.BlockSpec(memory_space=pltpu.HBM)
    bf16 = jnp.bfloat16
    dma = pltpu.SemaphoreType.DMA
    terms = pl.pallas_call(
        functools.partial(kernel, (S, F, C, A, T, K, NB, H)),
        out_shape=jax.ShapeDtypeStruct((NF // 2, parts, per, width // S), bf16),
        in_specs=[hbm] * 9,
        out_specs=pl.BlockSpec(memory_space=pl.ANY),
        scratch_shapes=[
            pltpu.VMEM((NB, height, T), bf16),
            pltpu.VMEM((C, S, A, T, T), bf16),
            pltpu.VMEM((C, total, T), bf16),
            pltpu.VMEM((C, F // 2, H, per // H, T), bf16),
            pltpu.VMEM((K * T, T), bf16),
            pltpu.VMEM((T, K * T), bf16),
            pltpu.VMEM((NF, width), jnp.int32),
            pltpu.VMEM((NF, total), jnp.int32),
            pltpu.VMEM((NT, T, T), bf16),
            pltpu.VMEM((NT, T, T), bf16),
            pltpu.VMEM((height, T), bf16),
            pltpu.SMEM((K, NF, NB), jnp.int32),
            pltpu.SMEM((K, NF, NB), jnp.int32),
            pltpu.SMEM((NF, K), jnp.int32),
            pltpu.SMEM((NF, K), jnp.int32),
            pltpu.VMEM((height, width), bf16),
        ]
        + [pltpu.VMEM((NB, T, T), bf16) for _ in range(C)]
        + [dma((8,)), dma((8,)), dma((C, S)), dma((C, S))]
        + [dma((C, F // 2, H)) for _ in range(4)],
        compiler_params=pltpu.CompilerParams(collective_id=0, has_side_effects=True, vmem_limit_bytes=67043328),
        name="sigma",
    )(amplitudes, beta_flip, alpha_flip, beta_tiles, alpha_tiles, *ids)
    return jnp.sum(terms.astype(jnp.float32), axis=0)


def solution(mesh):
    return jax.shard_map(
        functools.partial(local, mesh.shape["str"], mesh.shape["fac"]),
        mesh=mesh,
        in_specs=(P(None, "str", None), P(), P(), P(), P(), P(), P(), P(), P()),
        out_specs=P(None, "fac", "str"),
        check_vma=False,
    )
```

profile of v0, /device:TPU:0, one launch (start us, length us, event | category | flops | bytes accessed | tf_op | source)
XLA Modules:
  0.0 115.8 jit_solution(3004181289544244895)
XLA Ops:
  0.0 111.6 %sigma.1 = bf16[1,2,1024,512]{3,2,1,0:T(8,128)(2,1)} custom-call(bf16[2,512,4096]{2,1,0:T(8,128)(2,1)} %amp_hbm.1, s32[2,4096]{1,0:T(2,128)} %bflip_hbm.1, s32[2,4096]{1,0:T(2,128)} %aflip_hbm.1, bf16[16,128,128]{2,1,0:T(8,128)(2,1)} %btab_hbm.1, bf16[16,128,128]{2,1,0:T(8,128)(2,1)} %atab_hbm.1, s32[12,2,32]{2,1,0:T(2,128)} %bitcast.5, ...), custom_call_target="tpu_custom_call" | custom-call | tf_op jit(solution)/shard_map/sigma/pallas_call | solution.py:274
  111.6 4.2 %bitcast_convert_fusion = f32[2,1024,512]{2,1,0:T(8,128)} fusion(bf16[1,2,1024,512]{3,2,1,0:T(8,128)(2,1)} %sigma.1), kind=kLoop, calls=%fused_computation | loop fusion | flops 1048576 | bytes 6291456 | tf_op jit(solution)/shard_map/reduce_sum | solution.py:303
where the time goes:
time: 116 us
  Pallas kernels  112 us (97%)
  other arithmetic  4.2 us (4%)
    pallas_call x1, Pallas kernels, local(): pl.pallas_call(functools.partial(kernel, (S, F, C, A, T, K, NB, H)), out_...  112 us
    reduce_sum x1, other arithmetic, local(): return jnp.sum(terms.astype(jnp.float32), axis=0)  4.2 us

commit v1 on v0

--- a/solution.py
+++ b/solution.py
@@ -303,9 +303,481 @@
     return jnp.sum(terms.astype(jnp.float32), axis=0)
 
 
+def halves_kernel(dims, amp_hbm, bflip_hbm, aflip_hbm, btab_hbm, atab_hbm, bidx_hbm, aidx_hbm, btile_hbm, atile_hbm, out, far_out, *scratch):
+    S, F, C, A, T, K, NB, H = dims
+    amp, half_send, term_send, pair_recv, wb, wa, bflip, aflip, btab, atab, sign_a, sign_b, bidx, aidx, btile, atile, raw = scratch[:17]
+    recv = scratch[17 : 16 + C]
+    part_recv = scratch[16 + C : 18 + C]
+    a_sem, t_sem, s_send, s_recv, p_send, p_recv, f_send, f_recv, x_send, x_recv = scratch[18 + C :]
+    me = lax.axis_index("str")
+    pos = lax.axis_index("fac")
+    fac, part = split_position(pos, F)
+    chips = F // 2
+    chip = pos // 2
+    core = pos % 2
+    partner = chip * 2 + 1 - core
+    per = term_send.shape[1] // F
+    mid = S // 2
+    side = me // mid
+    first = side * mid
+    mirror = (1 - side) * mid + me % mid
+    last = C - 1
+
+    def far(t):
+        return (1 - side) * mid + (me + t) % mid
+
+    def near(t):
+        return first + (me + 1 + t) % mid
+
+    barrier = pltpu.get_barrier_semaphore()
+
+    def greet_str(t, _):
+        pl.semaphore_signal(barrier, inc=1, device_id={"str": (me + 1 + t) % S}, device_id_type=MESH)
+        return 0
+
+    def greet_fac(t, _):
+        peer = ((chip + 1 + t) % chips) * 2 + core
+        pl.semaphore_signal(barrier, inc=1, device_id={"fac": peer}, device_id_type=MESH)
+        pl.semaphore_signal(barrier, inc=1, device_id={"str": mirror, "fac": peer}, device_id_type=MESH)
+        return 0
+
+    lax.fori_loop(0, S - 1, greet_str, 0)
+    lax.fori_loop(0, chips - 1, greet_fac, 0)
+    pl.semaphore_signal(barrier, inc=1, device_id={"fac": partner}, device_id_type=MESH)
+
+    tables = [
+        pltpu.make_async_copy(src, dst, t_sem.at[n])
+        for n, (src, dst) in enumerate(
+            [
+                (bflip_hbm, bflip),
+                (aflip_hbm, aflip),
+                (btile_hbm, btile),
+                (bidx_hbm, bidx),
+                (btab_hbm, btab),
+                (atab_hbm, atab),
+                (aidx_hbm, aidx),
+                (atile_hbm, atile),
+            ]
+        )
+    ]
+
+    def load(a):
+        return pltpu.make_async_copy(amp_hbm.at[part, pl.ds(a * T, T)], raw.at[pl.ds(a * T, T)], a_sem.at[a])
+
+    for copy in tables[:5]:
+        copy.start()
+    for a in range(A):
+        load(a).start()
+    for copy in tables[5:]:
+        copy.start()
+
+    def signs(flips, start, size):
+        value = flips[:, pl.ds(start, size)]
+        mine = lax.broadcasted_iota(jnp.int32, value.shape, 0) == fac
+        return 1 - 2 * jnp.sum(jnp.where(mine, value.astype(jnp.float32), 0.0), axis=0, keepdims=True)
+
+    tables[0].wait()
+    sign_b[...] = jnp.broadcast_to(signs(bflip, 0, NB * T), sign_b.shape).astype(jnp.bfloat16)
+    tables[1].wait()
+    for a in range(A):
+        row = signs(aflip, pl.multiple_of((me * A + a) * T, T), T)
+        sign_a[pl.ds(a * T, T), :] = jnp.broadcast_to(row, (T, T)).T.astype(jnp.bfloat16)
+    tables[2].wait()
+    tables[3].wait()
+    tables[4].wait()
+    for s in range(K):
+        wb[pl.ds(s * T, T), :] = btab[btile[fac, s]].T
+    for m in range(2):
+        part_recv[m][mid * A] = jnp.zeros((T, T), jnp.bfloat16)
+
+    def str_copy(c, q, src):
+        return pltpu.make_async_remote_copy(
+            src_ref=half_send.at[c, q],
+            dst_ref=recv[c].at[pl.ds(src * A, A)],
+            send_sem=s_send.at[c, q],
+            recv_sem=s_recv.at[c, src],
+            device_id={"str": q},
+            device_id_type=MESH,
+        )
+
+    def strip_copy(q, a):
+        return pltpu.make_async_remote_copy(
+            src_ref=half_send.at[0, q, a],
+            dst_ref=recv[0].at[me * A + a],
+            send_sem=s_send.at[0, q],
+            recv_sem=s_recv.at[0, me],
+            device_id={"str": q},
+            device_id_type=MESH,
+        )
+
+    def owner(m, r):
+        return r if m == 0 else (1 - side) * mid + r % mid
+
+    def part_copy(m, r, src):
+        return pltpu.make_async_remote_copy(
+            src_ref=half_send.at[last, owner(m, r)],
+            dst_ref=part_recv[m].at[pl.ds(src % mid * A, A)],
+            send_sem=s_send.at[last, owner(m, r)],
+            recv_sem=s_recv.at[last, m * mid + src % mid],
+            device_id={"str": r},
+            device_id_type=MESH,
+        )
+
+    def sign(a):
+        load(a).wait()
+        rows = pl.ds(pl.multiple_of(a * T, T), T)
+        row_sign = sign_a[rows, :]
+        for k in range(NB):
+            column = jnp.broadcast_to(sign_b[:, k * T : (k + 1) * T].reshape(1, 16, T), (T // 16, 16, T)).reshape(T, T)
+            amp[k, rows, :] = raw[rows, k * T : (k + 1) * T] * column * row_sign
+
+    def strip(a):
+        rows = pl.ds(pl.multiple_of(a * T, T), T)
+        blocks = [jnp.concatenate([amp[bidx[s, fac, far(t) * C], rows, :] for s in range(K)], axis=1) for t in range(mid)]
+        res = jnp.dot(jnp.concatenate(blocks, axis=0), wb[...], preferred_element_type=jnp.float32).astype(jnp.bfloat16)
+        for t in range(mid):
+            half_send[0, far(t), a] = res[t * T : (t + 1) * T]
+
+    def send_strip(a):
+        for t in range(mid):
+            strip_copy(far(t), a).start()
+
+    sign(0)
+    strip(0)
+    pl.semaphore_wait(barrier, S - 1 + 2 * chips - 1)
+    send_strip(0)
+
+    def each_strip(a, _):
+        sign(a)
+        strip(a)
+        send_strip(a)
+        return 0
+
+    lax.fori_loop(1, A, each_strip, 0)
+
+    def beta(j):
+        lhs = jnp.concatenate([amp[bidx[s, fac, j]] for s in range(K)], axis=1)
+        res = jnp.dot(lhs, wb[...], preferred_element_type=jnp.float32)
+        return res.astype(jnp.bfloat16).reshape(A, T, T)
+
+    for m in (1, 0):
+
+        def near_part(t, _):
+            r = near(t)
+            half_send[last, owner(m, r)] = beta(owner(m, r) * C + last)
+            part_copy(m, r, me).start()
+            return 0
+
+        lax.fori_loop(0, mid - 1, near_part, 0)
+        part_recv[m][pl.ds(me % mid * A, A)] = beta(owner(m, me) * C + last)
+
+    for c in range(last):
+
+        def to_far(t, _):
+            q = far(t)
+            half_send[c, q] = beta(q * C + c)
+            str_copy(c, q, me).start()
+            return 0
+
+        def to_near(t, _):
+            q = near(t)
+            half_send[c, q] = beta(q * C + c)
+            str_copy(c, q, me).start()
+            return 0
+
+        if c > 0:
+            lax.fori_loop(0, mid, to_far, 0)
+        lax.fori_loop(0, mid - 1, to_near, 0)
+        recv[c][pl.ds(me * A, A)] = beta(me * C + c)
+
+    for copy in tables[5:]:
+        copy.wait()
+    for s in range(K):
+        wa[:, pl.ds(s * T, T)] = atab[atile[fac, s]]
+
+    piece = per // H
+    groups = chips * H
+
+    def place(g):
+        return (chip + 1 + g // H) % chips, g % H
+
+    def pair_copy(u, y, h, owner_core):
+        return pltpu.make_async_remote_copy(
+            src_ref=term_send.at[u, pl.ds((y * 2 + owner_core) * per + h * piece, piece)],
+            dst_ref=pair_recv.at[u, y, h],
+            send_sem=p_send.at[u, y, h],
+            recv_sem=p_recv.at[u, y, h],
+            device_id={"fac": partner},
+            device_id_type=MESH,
+        )
+
+    def fac_copy(c, y, h, src):
+        src_fac, src_part = split_position(src, F)
+        return pltpu.make_async_remote_copy(
+            src_ref=term_send.at[c, pl.ds((y * 2 + core) * per + h * piece, piece)],
+            dst_ref=out.at[src_fac // 2, src_part, pl.ds(h * piece, piece), pl.ds(c * T, T)],
+            send_sem=f_send.at[c, y, h],
+            recv_sem=f_recv.at[c, src // 2, h],
+            device_id={"fac": y * 2 + core},
+            device_id_type=MESH,
+        )
+
+    def far_copy(y, h, src):
+        src_fac, src_part = split_position(src, F)
+        return pltpu.make_async_remote_copy(
+            src_ref=term_send.at[C, pl.ds((y * 2 + core) * per + h * piece, piece)],
+            dst_ref=far_out.at[src_fac // 2, src_part, pl.ds(h * piece, piece)],
+            send_sem=x_send.at[y, h],
+            recv_sem=x_recv.at[src // 2, h],
+            device_id={"str": mirror, "fac": y * 2 + core},
+            device_id_type=MESH,
+        )
+
+    def own_copy(c):
+        return pltpu.make_async_copy(
+            term_send.at[c, pl.ds(pos * per, per)],
+            out.at[fac // 2, part, :, pl.ds(c * T, T)],
+            f_send.at[c, chip, 0],
+        )
+
+    def stage(u, gather, send, sent):
+        def alpha(i):
+            return jnp.dot(wa[...], gather(i), preferred_element_type=jnp.float32)
+
+        def store(i, value):
+            term_send[u, pl.ds(pl.multiple_of(i * T, T), T), :] = value.astype(jnp.bfloat16)
+
+        def for_partner(g):
+            y, h = place(g)
+
+            def block(b, _):
+                i = (y * 2 + 1 - core) * (per // T) + h * (piece // T) + b
+                store(i, alpha(i))
+                return 0
+
+            lax.fori_loop(0, piece // T, block, 0)
+            pair_copy(u, y, h, 1 - core).start()
+
+        def for_self(g):
+            y, h = place(g)
+            pair_copy(u, y, h, core).wait_recv()
+
+            def block(b, _):
+                i = (y * 2 + core) * (per // T) + h * (piece // T) + b
+                other = pair_recv[u, y, h, pl.ds(pl.multiple_of(b * T, T), T), :]
+                store(i, alpha(i) + other.astype(jnp.float32))
+                return 0
+
+            lax.fori_loop(0, piece // T, block, 0)
+
+        def away(g, _):
+            for_partner(g + 1)
+            for_self(g)
+            y, h = place(g)
+            send(y, h).start()
+            return 0
+
+        def home(g, _):
+            for_partner(g + 1)
+            for_self(g)
+            return 0
+
+        for_partner(0)
+        if sent == groups:
+            lax.fori_loop(0, groups - 1, away, 0)
+            for_self(groups - 1)
+            y, h = place(groups - 1)
+            send(y, h).start()
+        else:
+            lax.fori_loop(0, sent, away, 0)
+            lax.fori_loop(sent, groups - 1, home, 0)
+            for_self(groups - 1)
+
+    def gather_part(m):
+        def gather(i):
+            blocks = []
+            for s in range(K):
+                k = aidx[s, fac, i] - first * A
+                blocks.append(part_recv[m][jnp.where((k >= 0) & (k < mid * A), k, mid * A)])
+            return jnp.concatenate(blocks, axis=0)
+
+        return gather
+
+    def gather_full(c):
+        return lambda i: jnp.concatenate([recv[c][aidx[s, fac, i]] for s in range(K)], axis=0)
+
+    for m in (1, 0):
+
+        def arrive_part(t, _):
+            part_copy(m, me, near(t)).wait_recv()
+            return 0
+
+        lax.fori_loop(0, mid - 1, arrive_part, 0)
+        if m == 1:
+            stage(C, gather_part(1), lambda y, h: far_copy(y, h, pos), groups)
+        else:
+            stage(last, gather_part(0), lambda y, h: fac_copy(last, y, h, pos), groups - H)
+            own_copy(last).start()
+
+    for c in range(last):
+
+        def arrive(t, _):
+            src = (me + 1 + t) % S
+            str_copy(c, src, src).wait_recv()
+            return 0
+
+        lax.fori_loop(0, S - 1, arrive, 0)
+        stage(c, gather_full(c), lambda y, h: fac_copy(c, y, h, pos), groups - H)
+        own_copy(c).start()
+
+    for c in range(last):
+
+        def finish_str(t, _):
+            str_copy(c, (me + 1 + t) % S, me).wait_send()
+            return 0
+
+        lax.fori_loop(0, S - 1, finish_str, 0)
+
+    for m in range(2):
+
+        def finish_part(t, _):
+            part_copy(m, near(t), me).wait_send()
+            return 0
+
+        lax.fori_loop(0, mid - 1, finish_part, 0)
+
+    for u in range(C + 1):
+
+        def finish_pair(g, _):
+            y, h = place(g)
+            pair_copy(u, y, h, 1 - core).wait_send()
+            return 0
+
+        lax.fori_loop(0, groups, finish_pair, 0)
+
+    for c in range(C):
+
+        def finish_fac(g, _):
+            y, h = place(g)
+            fac_copy(c, y, h, pos).wait_send()
+            fac_copy(c, y, h, y * 2 + core).wait_recv()
+            return 0
+
+        lax.fori_loop(0, groups - H, finish_fac, 0)
+        own_copy(c).wait()
+
+    def finish_far(g, _):
+        y, h = place(g)
+        far_copy(y, h, pos).wait_send()
+        far_copy(y, h, y * 2 + core).wait_recv()
+        return 0
+
+    lax.fori_loop(0, groups, finish_far, 0)
+
+
+def finish_kernel(T, rows, terms, far, out, wide, sem):
+    slots, parts, per, width = terms.shape
+    count = per // rows
+
+    def copy(p, r):
+        block = pl.ds(pl.multiple_of(r * rows, rows), rows)
+        return pltpu.make_async_copy(wide.at[p, block], out.at[p, block], sem.at[p, r])
+
+    for p in range(parts):
+
+        def convert(r, _):
+            block = pl.ds(pl.multiple_of(r * rows, rows), rows)
+            value = sum(terms[n, p, block, :].astype(jnp.float32) for n in range(slots))
+            tail = sum(far[n, p, block, :].astype(jnp.float32) for n in range(slots))
+            wide[p, block, : width - T] = value[:, : width - T]
+            wide[p, block, width - T :] = value[:, width - T :] + tail
+            copy(p, r).start()
+            return 0
+
+        lax.fori_loop(0, count, convert, 0)
+
+    for p in range(parts):
+
+        def wait(r, _):
+            copy(p, r).wait()
+            return 0
+
+        lax.fori_loop(0, count, wait, 0)
+
+
+def halves(S, F, amplitudes, beta_index, beta_tile, beta_flip, alpha_index, alpha_tile, alpha_flip, beta_tiles, alpha_tiles):
+    NF, NB, K = beta_index.shape
+    NT, T, _ = beta_tiles.shape
+    parts, height, width = amplitudes.shape
+    total = height * S
+    A = height // T
+    C = width // S // T
+    mid = S // 2
+    assert F == 2 * NF and parts == 2 and NF % 2 == 0 and height % T == 0 and S % 2 == 0
+    per = total // F
+    H = math.gcd(per // T, 4)
+    ids = (beta_index.transpose(2, 0, 1), alpha_index.transpose(2, 0, 1), beta_tile, alpha_tile)
+    hbm = pl.BlockSpec(memory_space=pltpu.HBM)
+    vmem = pl.BlockSpec(memory_space=pltpu.VMEM)
+    bf16 = jnp.bfloat16
+    dma = pltpu.SemaphoreType.DMA
+    terms, far = pl.pallas_call(
+        functools.partial(halves_kernel, (S, F, C, A, T, K, NB, H)),
+        out_shape=(
+            pltpu.VMEM((NF // 2, parts, per, width // S), bf16),
+            pltpu.VMEM((NF // 2, parts, per, T), bf16),
+        ),
+        in_specs=[hbm] * 9,
+        out_specs=(vmem, vmem),
+        scratch_shapes=[
+            pltpu.VMEM((NB, height, T), bf16),
+            pltpu.VMEM((C, S, A, T, T), bf16),
+            pltpu.VMEM((C + 1, total, T), bf16),
+            pltpu.VMEM((C + 1, F // 2, H, per // H, T), bf16),
+            pltpu.VMEM((K * T, T), bf16),
+            pltpu.VMEM((T, K * T), bf16),
+            pltpu.VMEM((NF, width), jnp.int32),
+            pltpu.VMEM((NF, total), jnp.int32),
+            pltpu.VMEM((NT, T, T), bf16),
+            pltpu.VMEM((NT, T, T), bf16),
+            pltpu.VMEM((height, T), bf16),
+            pltpu.VMEM((16, width), bf16),
+            pltpu.SMEM((K, NF, NB), jnp.int32),
+            pltpu.SMEM((K, NF, NB), jnp.int32),
+            pltpu.SMEM((NF, K), jnp.int32),
+            pltpu.SMEM((NF, K), jnp.int32),
+            pltpu.VMEM((height, width), bf16),
+        ]
+        + [pltpu.VMEM((NB, T, T), bf16) for _ in range(C - 1)]
+        + [pltpu.VMEM((mid * A + 1, T, T), bf16) for _ in range(2)]
+        + [dma((A,)), dma((8,)), dma((C, S)), dma((C, S))]
+        + [dma((C + 1, F // 2, H)) for _ in range(2)]
+        + [dma((C, F // 2, H)) for _ in range(2)]
+        + [dma((F // 2, H)) for _ in range(2)],
+        compiler_params=pltpu.CompilerParams(collective_id=0, has_side_effects=True, vmem_limit_bytes=48 << 20),
+        name="sigma",
+    )(*[pltpu.with_memory_space_constraint(x, pltpu.HBM) for x in (amplitudes, beta_flip, alpha_flip, beta_tiles, alpha_tiles, *ids)])
+    rows = math.gcd(per, 128)
+    return pl.pallas_call(
+        functools.partial(finish_kernel, T, rows),
+        out_shape=jax.ShapeDtypeStruct((parts, per, width // S), jnp.float32),
+        in_specs=[vmem, vmem],
+        out_specs=pl.BlockSpec(memory_space=pltpu.HBM),
+        scratch_shapes=[pltpu.VMEM((parts, per, width // S), jnp.float32), dma((parts, per // rows))],
+        compiler_params=pltpu.CompilerParams(vmem_limit_bytes=16 << 20),
+        name="finish",
+    )(terms, far)
+
+
+def either(S, F, *args):
+    height, width, T = args[0].shape[1], args[0].shape[2], args[7].shape[1]
+    form = halves if width // S >= 2 * T and height % T == 0 and S % 2 == 0 else local
+    return form(S, F, *args)
+
+
 def solution(mesh):
     return jax.shard_map(
-        functools.partial(local, mesh.shape["str"], mesh.shape["fac"]),
+        functools.partial(either, mesh.shape["str"], mesh.shape["fac"]),
         mesh=mesh,
         in_specs=(P(None, "str", None), P(), P(), P(), P(), P(), P(), P(), P()),
         out_specs=P(None, "fac", "str"),

time: 116 us -> 105 us (0.905)
  Pallas kernels: 112 us -> 105 us
  other arithmetic: 4.2 us -> 0 us
    pallas_call x1 -> x2, Pallas kernels: 112 us -> 105 us  [the longest x1 102 us: halves(): pl.pallas_call(functools.partial(halves_kernel, (S, F, C, A, T, K, NB, H)...]
    reduce_sum x1 -> x0, other arithmetic: 4.2 us -> none  [local(): return jnp.sum(terms.astype(jnp.float32), axis=0)]
where the time goes in v1:
time: 105 us
  Pallas kernels  105 us (100%)
    pallas_call x1, Pallas kernels, halves(): pl.pallas_call(functools.partial(halves_kernel, (S, F, C, A, T, K, NB, H)...  102 us
    pallas_call x1, Pallas kernels, halves(): pl.pallas_call(functools.partial(finish_kernel, T, rows), out_shape=jax.S...  2.16 us

profile of v1, /device:TPU:0, one launch (start us, length us, event | category | flops | bytes accessed | tf_op | source)
XLA Modules:
  0.0 104.5 jit_solution(11986430634879856678)
XLA Ops:
  0.0 102.4 %sigma.1 = (bf16[1,2,1024,512]{3,2,1,0:T(8,128)(2,1)S(1)}, bf16[1,2,1024,128]{3,2,1,0:T(8,128)(2,1)S(1)}) custom-call(bf16[2,512,4096]{2,1,0:T(8,128)(2,1)} %amp_hbm.1, s32[2,4096]{1,0:T(2,128)} %bflip_hbm.1, s32[2,4096]{1,0:T(2,128)} %aflip_hbm.1, bf16[16,128,128]{2,1,0:T(8,128)(2,1)} %btab_hbm.1, bf16[16,128,128]{2,1,0:T(8,128)(2,1)} %atab_hbm.1, ...), custom_call_target="tpu_custom_call" | custom-call | tf_op jit(solution)/shard_map/sigma/pallas_call | solution.py:724
  102.4 2.2 %finish.1 = f32[2,1024,512]{2,1,0:T(8,128)} custom-call(bf16[1,2,1024,512]{3,2,1,0:T(8,128)(2,1)S(1)} %get-tuple-element.7.terms, bf16[1,2,1024,128]{3,2,1,0:T(8,128)(2,1)S(1)} %get-tuple-element.8.far), custom_call_target="tpu_custom_call" | custom-call | tf_op jit(solution)/shard_map/finish/pallas_call | solution.py:761

commit v2 on v1

--- a/solution.py
+++ b/solution.py
@@ -308,7 +308,7 @@
     amp, half_send, term_send, pair_recv, wb, wa, bflip, aflip, btab, atab, sign_a, sign_b, bidx, aidx, btile, atile, raw = scratch[:17]
     recv = scratch[17 : 16 + C]
     part_recv = scratch[16 + C : 18 + C]
-    a_sem, t_sem, s_send, s_recv, p_send, p_recv, f_send, f_recv, x_send, x_recv = scratch[18 + C :]
+    a_sem, t_sem, s_send, s_recv, p_send, p_recv, f_sem, x_sem = scratch[18 + C :]
     me = lax.axis_index("str")
     pos = lax.axis_index("fac")
     fac, part = split_position(pos, F)
@@ -390,22 +390,28 @@
     for m in range(2):
         part_recv[m][mid * A] = jnp.zeros((T, T), jnp.bfloat16)
 
-    def str_copy(c, q, src):
-        return pltpu.make_async_remote_copy(
-            src_ref=half_send.at[c, q],
-            dst_ref=recv[c].at[pl.ds(src * A, A)],
-            send_sem=s_send.at[c, q],
-            recv_sem=s_recv.at[c, src],
+    def slot(c, q):
+        return c * (S - 1) + (q - me - 1 + S) % S
+
+    def wait_bytes(ref, sem):
+        pltpu.make_async_copy(ref, ref, sem).wait()
+
+    def str_copy(c, q):
+        return pltpu.make_async_remote_copy(
+            src_ref=half_send.at[slot(c, q)],
+            dst_ref=recv[c].at[pl.ds(me * A, A)],
+            send_sem=s_send,
+            recv_sem=s_recv.at[c],
             device_id={"str": q},
             device_id_type=MESH,
         )
 
     def strip_copy(q, a):
         return pltpu.make_async_remote_copy(
-            src_ref=half_send.at[0, q, a],
+            src_ref=half_send.at[slot(0, q), a],
             dst_ref=recv[0].at[me * A + a],
-            send_sem=s_send.at[0, q],
-            recv_sem=s_recv.at[0, me],
+            send_sem=s_send,
+            recv_sem=s_recv.at[0],
             device_id={"str": q},
             device_id_type=MESH,
         )
@@ -413,13 +419,13 @@
     def owner(m, r):
         return r if m == 0 else (1 - side) * mid + r % mid
 
-    def part_copy(m, r, src):
-        return pltpu.make_async_remote_copy(
-            src_ref=half_send.at[last, owner(m, r)],
-            dst_ref=part_recv[m].at[pl.ds(src % mid * A, A)],
-            send_sem=s_send.at[last, owner(m, r)],
-            recv_sem=s_recv.at[last, m * mid + src % mid],
-            device_id={"str": r},
+    def part_copy(m, t):
+        return pltpu.make_async_remote_copy(
+            src_ref=half_send.at[last * (S - 1) + m * (mid - 1) + t],
+            dst_ref=part_recv[m].at[pl.ds(me % mid * A, A)],
+            send_sem=s_send,
+            recv_sem=s_recv.at[last + m],
+            device_id={"str": near(t)},
             device_id_type=MESH,
         )
 
@@ -436,7 +442,7 @@
         blocks = [jnp.concatenate([amp[bidx[s, fac, far(t) * C], rows, :] for s in range(K)], axis=1) for t in range(mid)]
         res = jnp.dot(jnp.concatenate(blocks, axis=0), wb[...], preferred_element_type=jnp.float32).astype(jnp.bfloat16)
         for t in range(mid):
-            half_send[0, far(t), a] = res[t * T : (t + 1) * T]
+            half_send[slot(0, far(t)), a] = res[t * T : (t + 1) * T]
 
     def send_strip(a):
         for t in range(mid):
@@ -463,9 +469,8 @@
     for m in (1, 0):
 
         def near_part(t, _):
-            r = near(t)
-            half_send[last, owner(m, r)] = beta(owner(m, r) * C + last)
-            part_copy(m, r, me).start()
+            half_send[last * (S - 1) + m * (mid - 1) + t] = beta(owner(m, near(t)) * C + last)
+            part_copy(m, t).start()
             return 0
 
         lax.fori_loop(0, mid - 1, near_part, 0)
@@ -475,14 +480,14 @@
 
         def to_far(t, _):
             q = far(t)
-            half_send[c, q] = beta(q * C + c)
-            str_copy(c, q, me).start()
+            half_send[slot(c, q)] = beta(q * C + c)
+            str_copy(c, q).start()
             return 0
 
         def to_near(t, _):
             q = near(t)
-            half_send[c, q] = beta(q * C + c)
-            str_copy(c, q, me).start()
+            half_send[slot(c, q)] = beta(q * C + c)
+            str_copy(c, q).start()
             return 0
 
         if c > 0:
@@ -501,43 +506,37 @@
     def place(g):
         return (chip + 1 + g // H) % chips, g % H
 
+    def turn(u):
+        return {C: 0, last: 1}.get(u, u + 2)
+
     def pair_copy(u, y, h, owner_core):
         return pltpu.make_async_remote_copy(
             src_ref=term_send.at[u, pl.ds((y * 2 + owner_core) * per + h * piece, piece)],
             dst_ref=pair_recv.at[u, y, h],
-            send_sem=p_send.at[u, y, h],
-            recv_sem=p_recv.at[u, y, h],
+            send_sem=p_send,
+            recv_sem=p_recv.at[turn(u) % 2, y, h],
             device_id={"fac": partner},
             device_id_type=MESH,
         )
 
-    def fac_copy(c, y, h, src):
-        src_fac, src_part = split_position(src, F)
+    def fac_copy(c, y, h):
         return pltpu.make_async_remote_copy(
             src_ref=term_send.at[c, pl.ds((y * 2 + core) * per + h * piece, piece)],
-            dst_ref=out.at[src_fac // 2, src_part, pl.ds(h * piece, piece), pl.ds(c * T, T)],
-            send_sem=f_send.at[c, y, h],
-            recv_sem=f_recv.at[c, src // 2, h],
+            dst_ref=out.at[fac // 2, part, pl.ds(h * piece, piece), pl.ds(c * T, T)],
+            send_sem=f_sem.at[0],
+            recv_sem=f_sem.at[1],
             device_id={"fac": y * 2 + core},
             device_id_type=MESH,
         )
 
-    def far_copy(y, h, src):
-        src_fac, src_part = split_position(src, F)
+    def far_copy(y, h):
         return pltpu.make_async_remote_copy(
             src_ref=term_send.at[C, pl.ds((y * 2 + core) * per + h * piece, piece)],
-            dst_ref=far_out.at[src_fac // 2, src_part, pl.ds(h * piece, piece)],
-            send_sem=x_send.at[y, h],
-            recv_sem=x_recv.at[src // 2, h],
+            dst_ref=far_out.at[fac // 2, part, pl.ds(h * piece, piece)],
+            send_sem=x_sem.at[0],
+            recv_sem=x_sem.at[1],
             device_id={"str": mirror, "fac": y * 2 + core},
             device_id_type=MESH,
-        )
-
-    def own_copy(c):
-        return pltpu.make_async_copy(
-            term_send.at[c, pl.ds(pos * per, per)],
-            out.at[fac // 2, part, :, pl.ds(c * T, T)],
-            f_send.at[c, chip, 0],
         )
 
     def stage(u, gather, send, sent):
@@ -558,40 +557,44 @@
             lax.fori_loop(0, piece // T, block, 0)
             pair_copy(u, y, h, 1 - core).start()
 
-        def for_self(g):
+        def for_self(g, home):
             y, h = place(g)
             pair_copy(u, y, h, core).wait_recv()
 
             def block(b, _):
                 i = (y * 2 + core) * (per // T) + h * (piece // T) + b
                 other = pair_recv[u, y, h, pl.ds(pl.multiple_of(b * T, T), T), :]
-                store(i, alpha(i) + other.astype(jnp.float32))
+                value = alpha(i) + other.astype(jnp.float32)
+                if home:
+                    rows = pl.ds(pl.multiple_of(h * piece + b * T, T), T)
+                    out[fac // 2, part, rows, u * T : (u + 1) * T] = value.astype(jnp.bfloat16)
+                else:
+                    store(i, value)
                 return 0
 
             lax.fori_loop(0, piece // T, block, 0)
 
         def away(g, _):
             for_partner(g + 1)
-            for_self(g)
+            for_self(g, False)
             y, h = place(g)
             send(y, h).start()
             return 0
 
         def home(g, _):
             for_partner(g + 1)
-            for_self(g)
+            for_self(g, True)
             return 0
 
         for_partner(0)
-        if sent == groups:
-            lax.fori_loop(0, groups - 1, away, 0)
-            for_self(groups - 1)
+        lax.fori_loop(0, min(sent, groups - 1), away, 0)
+        if sent < groups:
+            lax.fori_loop(sent, groups - 1, home, 0)
+            for_self(groups - 1, True)
+        else:
+            for_self(groups - 1, False)
             y, h = place(groups - 1)
             send(y, h).start()
-        else:
-            lax.fori_loop(0, sent, away, 0)
-            lax.fori_loop(sent, groups - 1, home, 0)
-            for_self(groups - 1)
 
     def gather_part(m):
         def gather(i):
@@ -607,72 +610,21 @@
         return lambda i: jnp.concatenate([recv[c][aidx[s, fac, i]] for s in range(K)], axis=0)
 
     for m in (1, 0):
-
-        def arrive_part(t, _):
-            part_copy(m, me, near(t)).wait_recv()
-            return 0
-
-        lax.fori_loop(0, mid - 1, arrive_part, 0)
+        wait_bytes(part_recv[m].at[pl.ds(0, (mid - 1) * A)], s_recv.at[last + m])
         if m == 1:
-            stage(C, gather_part(1), lambda y, h: far_copy(y, h, pos), groups)
+            stage(C, gather_part(1), far_copy, groups)
         else:
-            stage(last, gather_part(0), lambda y, h: fac_copy(last, y, h, pos), groups - H)
-            own_copy(last).start()
+            stage(last, gather_part(0), lambda y, h: fac_copy(last, y, h), groups - H)
 
     for c in range(last):
-
-        def arrive(t, _):
-            src = (me + 1 + t) % S
-            str_copy(c, src, src).wait_recv()
-            return 0
-
-        lax.fori_loop(0, S - 1, arrive, 0)
-        stage(c, gather_full(c), lambda y, h: fac_copy(c, y, h, pos), groups - H)
-        own_copy(c).start()
-
-    for c in range(last):
-
-        def finish_str(t, _):
-            str_copy(c, (me + 1 + t) % S, me).wait_send()
-            return 0
-
-        lax.fori_loop(0, S - 1, finish_str, 0)
-
-    for m in range(2):
-
-        def finish_part(t, _):
-            part_copy(m, near(t), me).wait_send()
-            return 0
-
-        lax.fori_loop(0, mid - 1, finish_part, 0)
-
-    for u in range(C + 1):
-
-        def finish_pair(g, _):
-            y, h = place(g)
-            pair_copy(u, y, h, 1 - core).wait_send()
-            return 0
-
-        lax.fori_loop(0, groups, finish_pair, 0)
-
-    for c in range(C):
-
-        def finish_fac(g, _):
-            y, h = place(g)
-            fac_copy(c, y, h, pos).wait_send()
-            fac_copy(c, y, h, y * 2 + core).wait_recv()
-            return 0
-
-        lax.fori_loop(0, groups - H, finish_fac, 0)
-        own_copy(c).wait()
-
-    def finish_far(g, _):
-        y, h = place(g)
-        far_copy(y, h, pos).wait_send()
-        far_copy(y, h, y * 2 + core).wait_recv()
-        return 0
-
-    lax.fori_loop(0, groups, finish_far, 0)
+        wait_bytes(recv[c].at[pl.ds(0, (S - 1) * A)], s_recv.at[c])
+        stage(c, gather_full(c), lambda y, h: fac_copy(c, y, h), groups - H)
+
+    wait_bytes(half_send, s_send)
+    wait_bytes(pair_recv, p_send)
+    for n in range(2):
+        wait_bytes(pair_recv.at[pl.ds(0, C), pl.ds(0, chips - 1)], f_sem.at[n])
+        wait_bytes(pair_recv.at[0], x_sem.at[n])
 
 
 def finish_kernel(T, rows, terms, far, out, wide, sem):
@@ -731,7 +683,7 @@
         out_specs=(vmem, vmem),
         scratch_shapes=[
             pltpu.VMEM((NB, height, T), bf16),
-            pltpu.VMEM((C, S, A, T, T), bf16),
+            pltpu.VMEM(((C - 1) * (S - 1) + 2 * (mid - 1), A, T, T), bf16),
             pltpu.VMEM((C + 1, total, T), bf16),
             pltpu.VMEM((C + 1, F // 2, H, per // H, T), bf16),
             pltpu.VMEM((K * T, T), bf16),
@@ -750,10 +702,7 @@
         ]
         + [pltpu.VMEM((NB, T, T), bf16) for _ in range(C - 1)]
         + [pltpu.VMEM((mid * A + 1, T, T), bf16) for _ in range(2)]
-        + [dma((A,)), dma((8,)), dma((C, S)), dma((C, S))]
-        + [dma((C + 1, F // 2, H)) for _ in range(2)]
-        + [dma((C, F // 2, H)) for _ in range(2)]
-        + [dma((F // 2, H)) for _ in range(2)],
+        + [dma((A,)), dma((8,)), dma, dma((C + 1,)), dma, dma((2, F // 2, H)), dma((2,)), dma((2,))],
         compiler_params=pltpu.CompilerParams(collective_id=0, has_side_effects=True, vmem_limit_bytes=48 << 20),
         name="sigma",
     )(*[pltpu.with_memory_space_constraint(x, pltpu.HBM) for x in (amplitudes, beta_flip, alpha_flip, beta_tiles, alpha_tiles, *ids)])

time: 105 us -> 102 us (0.971)
  Pallas kernels: 105 us -> 101 us
    pallas_call x1, Pallas kernels: 102 us -> 99.2 us  [halves(): pl.pallas_call(functools.partial(halves_kernel, (S, F, C, A, T, K, NB, H)...]
where the time goes in v2:
time: 102 us; the launch traced here: 101 us
  Pallas kernels  101 us (99%)
    pallas_call x1, Pallas kernels, halves(): pl.pallas_call(functools.partial(halves_kernel, (S, F, C, A, T, K, NB, H)...  99.2 us
    pallas_call x1, Pallas kernels, halves(): pl.pallas_call(functools.partial(finish_kernel, T, rows), out_shape=jax.S...  2.16 us

profile of v2, /device:TPU:0, one launch (start us, length us, event | category | flops | bytes accessed | tf_op | source)
XLA Modules:
  0.0 101.4 jit_solution(440972909271296192)
XLA Ops:
  0.0 99.2 %sigma.1 = (bf16[1,2,1024,512]{3,2,1,0:T(8,128)(2,1)S(1)}, bf16[1,2,1024,128]{3,2,1,0:T(8,128)(2,1)S(1)}) custom-call(bf16[2,512,4096]{2,1,0:T(8,128)(2,1)} %amp_hbm.1, s32[2,4096]{1,0:T(2,128)} %bflip_hbm.1, s32[2,4096]{1,0:T(2,128)} %aflip_hbm.1, bf16[16,128,128]{2,1,0:T(8,128)(2,1)} %btab_hbm.1, bf16[16,128,128]{2,1,0:T(8,128)(2,1)} %atab_hbm.1, ...), custom_call_target="tpu_custom_call" | custom-call | tf_op jit(solution)/shard_map/sigma/pallas_call | solution.py:676
  99.2 2.2 %finish.1 = f32[2,1024,512]{2,1,0:T(8,128)} custom-call(bf16[1,2,1024,512]{3,2,1,0:T(8,128)(2,1)S(1)} %get-tuple-element.7.terms, bf16[1,2,1024,128]{3,2,1,0:T(8,128)(2,1)S(1)} %get-tuple-element.8.far), custom_call_target="tpu_custom_call" | custom-call | tf_op jit(solution)/shard_map/finish/pallas_call | solution.py:710

commit v3 on v2

--- a/solution.py
+++ b/solution.py
@@ -306,9 +306,10 @@
 def halves_kernel(dims, amp_hbm, bflip_hbm, aflip_hbm, btab_hbm, atab_hbm, bidx_hbm, aidx_hbm, btile_hbm, atile_hbm, out, far_out, *scratch):
     S, F, C, A, T, K, NB, H = dims
     amp, half_send, term_send, pair_recv, wb, wa, bflip, aflip, btab, atab, sign_a, sign_b, bidx, aidx, btile, atile, raw = scratch[:17]
-    recv = scratch[17 : 16 + C]
-    part_recv = scratch[16 + C : 18 + C]
-    a_sem, t_sem, s_send, s_recv, p_send, p_recv, f_sem, x_sem = scratch[18 + C :]
+    D = C // 2
+    recv = scratch[17 : 17 + D]
+    part_recv = (scratch[17 + D : 17 + 2 * D], scratch[17 + 2 * D : 17 + 3 * D])
+    a_sem, t_sem, s_send, s_recv, p_send, p_recv, f_sem, x_sem = scratch[17 + 3 * D :]
     me = lax.axis_index("str")
     pos = lax.axis_index("fac")
     fac, part = split_position(pos, F)
@@ -320,14 +321,23 @@
     mid = S // 2
     side = me // mid
     first = side * mid
-    mirror = (1 - side) * mid + me % mid
-    last = C - 1
+    def swap(r, t, flip):
+        place = (r + mid // 2 * (1 - t % 2)) % mid
+        return place + flip * (mid - 1 - 2 * place)
+
+    def opposite(r):
+        return (1 - side) * mid + (r + mid // 2) % mid
+
+    late = (me < mid // 2) | (me >= S - mid // 2)
+
 
     def far(t):
-        return (1 - side) * mid + (me + t) % mid
+        at = swap(me, t, t // 2) if mid == 4 else (me + t) % mid
+        return (1 - side) * mid + at
 
     def near(t):
-        return first + (me + 1 + t) % mid
+        at = swap(me, t, (t + 1) // 2) if mid == 4 else (me + 1 + t) % mid
+        return first + at
 
     barrier = pltpu.get_barrier_semaphore()
 
@@ -338,7 +348,7 @@
     def greet_fac(t, _):
         peer = ((chip + 1 + t) % chips) * 2 + core
         pl.semaphore_signal(barrier, inc=1, device_id={"fac": peer}, device_id_type=MESH)
-        pl.semaphore_signal(barrier, inc=1, device_id={"str": mirror, "fac": peer}, device_id_type=MESH)
+        pl.semaphore_signal(barrier, inc=1, device_id={"str": opposite(me), "fac": peer}, device_id_type=MESH)
         return 0
 
     lax.fori_loop(0, S - 1, greet_str, 0)
@@ -388,7 +398,8 @@
     for s in range(K):
         wb[pl.ds(s * T, T), :] = btab[btile[fac, s]].T
     for m in range(2):
-        part_recv[m][mid * A] = jnp.zeros((T, T), jnp.bfloat16)
+        for d in range(D):
+            part_recv[m][d][mid * A] = jnp.zeros((T, T), jnp.bfloat16)
 
     def slot(c, q):
         return c * (S - 1) + (q - me - 1 + S) % S
@@ -417,14 +428,17 @@
         )
 
     def owner(m, r):
-        return r if m == 0 else (1 - side) * mid + r % mid
-
-    def part_copy(m, t):
-        return pltpu.make_async_remote_copy(
-            src_ref=half_send.at[last * (S - 1) + m * (mid - 1) + t],
-            dst_ref=part_recv[m].at[pl.ds(me % mid * A, A)],
+        return r if m == 0 else opposite(r)
+
+    def part_slot(m, d, t):
+        return D * (S - 1) + (m * D + d) * (mid - 1) + t
+
+    def part_copy(m, d, t):
+        return pltpu.make_async_remote_copy(
+            src_ref=half_send.at[part_slot(m, d, t)],
+            dst_ref=part_recv[m][d].at[pl.ds(me % mid * A, A)],
             send_sem=s_send,
-            recv_sem=s_recv.at[last + m],
+            recv_sem=s_recv.at[D + m * D + d],
             device_id={"str": near(t)},
             device_id_type=MESH,
         )
@@ -466,34 +480,33 @@
         res = jnp.dot(lhs, wb[...], preferred_element_type=jnp.float32)
         return res.astype(jnp.bfloat16).reshape(A, T, T)
 
-    for m in (1, 0):
-
+    def spread_part(m, d):
         def near_part(t, _):
-            half_send[last * (S - 1) + m * (mid - 1) + t] = beta(owner(m, near(t)) * C + last)
-            part_copy(m, t).start()
+            half_send[part_slot(m, d, t)] = beta(owner(m, near(t)) * C + D + d)
+            part_copy(m, d, t).start()
             return 0
 
         lax.fori_loop(0, mid - 1, near_part, 0)
-        part_recv[m][pl.ds(me % mid * A, A)] = beta(owner(m, me) * C + last)
-
-    for c in range(last):
-
-        def to_far(t, _):
-            q = far(t)
+        part_recv[m][d][pl.ds(me % mid * A, A)] = beta(owner(m, me) * C + D + d)
+
+    def spread(c, dest, count):
+        def one(t, _):
+            q = dest(t)
             half_send[slot(c, q)] = beta(q * C + c)
             str_copy(c, q).start()
             return 0
 
-        def to_near(t, _):
-            q = near(t)
-            half_send[slot(c, q)] = beta(q * C + c)
-            str_copy(c, q).start()
-            return 0
-
+        lax.fori_loop(0, count, one, 0)
+
+    for d in range(D):
+        spread_part(1, d)
+    for c in range(D):
         if c > 0:
-            lax.fori_loop(0, mid, to_far, 0)
-        lax.fori_loop(0, mid - 1, to_near, 0)
+            spread(c, far, mid)
+        spread(c, near, mid - 1)
         recv[c][pl.ds(me * A, A)] = beta(me * C + c)
+    for d in range(D):
+        spread_part(0, d)
 
     for copy in tables[5:]:
         copy.wait()
@@ -503,43 +516,43 @@
     piece = per // H
     groups = chips * H
 
-    def place(g):
-        return (chip + 1 + g // H) % chips, g % H
-
-    def turn(u):
-        return {C: 0, last: 1}.get(u, u + 2)
-
     def pair_copy(u, y, h, owner_core):
         return pltpu.make_async_remote_copy(
             src_ref=term_send.at[u, pl.ds((y * 2 + owner_core) * per + h * piece, piece)],
             dst_ref=pair_recv.at[u, y, h],
             send_sem=p_send,
-            recv_sem=p_recv.at[turn(u) % 2, y, h],
+            recv_sem=p_recv.at[u % 2, y, h],
             device_id={"fac": partner},
             device_id_type=MESH,
         )
 
-    def fac_copy(c, y, h):
-        return pltpu.make_async_remote_copy(
-            src_ref=term_send.at[c, pl.ds((y * 2 + core) * per + h * piece, piece)],
-            dst_ref=out.at[fac // 2, part, pl.ds(h * piece, piece), pl.ds(c * T, T)],
+    def far_copy(y, h):
+        return pltpu.make_async_remote_copy(
+            src_ref=term_send.at[0, pl.ds((y * 2 + core) * per + h * piece, piece)],
+            dst_ref=far_out.at[fac // 2, part, pl.ds(h * piece, piece)],
+            send_sem=x_sem.at[0],
+            recv_sem=x_sem.at[1],
+            device_id={"str": opposite(me), "fac": y * 2 + core},
+            device_id_type=MESH,
+        )
+
+    def columns(u):
+        return slice(D * T, C * T) if u == 2 else slice(0, D * T)
+
+    def fac_copy(u, y, h):
+        return pltpu.make_async_remote_copy(
+            src_ref=term_send.at[u, pl.ds((y * 2 + core) * per + h * piece, piece)],
+            dst_ref=out.at[fac // 2, part, pl.ds(h * piece, piece), columns(u)],
             send_sem=f_sem.at[0],
             recv_sem=f_sem.at[1],
             device_id={"fac": y * 2 + core},
             device_id_type=MESH,
         )
 
-    def far_copy(y, h):
-        return pltpu.make_async_remote_copy(
-            src_ref=term_send.at[C, pl.ds((y * 2 + core) * per + h * piece, piece)],
-            dst_ref=far_out.at[fac // 2, part, pl.ds(h * piece, piece)],
-            send_sem=x_sem.at[0],
-            recv_sem=x_sem.at[1],
-            device_id={"str": mirror, "fac": y * 2 + core},
-            device_id_type=MESH,
-        )
-
     def stage(u, gather, send, sent):
+        def place(g):
+            return (g // H if u == 0 else (chip + 1 + g // H) % chips), g % H
+
         def alpha(i):
             return jnp.dot(wa[...], gather(i), preferred_element_type=jnp.float32)
 
@@ -567,7 +580,7 @@
                 value = alpha(i) + other.astype(jnp.float32)
                 if home:
                     rows = pl.ds(pl.multiple_of(h * piece + b * T, T), T)
-                    out[fac // 2, part, rows, u * T : (u + 1) * T] = value.astype(jnp.bfloat16)
+                    out[fac // 2, part, rows, columns(u)] = value.astype(jnp.bfloat16)
                 else:
                     store(i, value)
                 return 0
@@ -578,7 +591,7 @@
             for_partner(g + 1)
             for_self(g, False)
             y, h = place(g)
-            send(y, h).start()
+            send(y, h)
             return 0
 
         def home(g, _):
@@ -594,42 +607,56 @@
         else:
             for_self(groups - 1, False)
             y, h = place(groups - 1)
-            send(y, h).start()
+            send(y, h)
+
+    def gather(buffers, index):
+        columns = [jnp.concatenate([buffer[index(s)] for s in range(K)], axis=0) for buffer in buffers]
+        return jnp.concatenate(columns, axis=1)
 
     def gather_part(m):
-        def gather(i):
-            blocks = []
-            for s in range(K):
-                k = aidx[s, fac, i] - first * A
-                blocks.append(part_recv[m][jnp.where((k >= 0) & (k < mid * A), k, mid * A)])
-            return jnp.concatenate(blocks, axis=0)
-
-        return gather
-
-    def gather_full(c):
-        return lambda i: jnp.concatenate([recv[c][aidx[s, fac, i]] for s in range(K)], axis=0)
-
-    for m in (1, 0):
-        wait_bytes(part_recv[m].at[pl.ds(0, (mid - 1) * A)], s_recv.at[last + m])
-        if m == 1:
-            stage(C, gather_part(1), far_copy, groups)
-        else:
-            stage(last, gather_part(0), lambda y, h: fac_copy(last, y, h), groups - H)
-
-    for c in range(last):
+        def index(s, i):
+            k = aidx[s, fac, i] - first * A
+            return jnp.where((k >= 0) & (k < mid * A), k, mid * A)
+
+        return lambda i: gather(part_recv[m], lambda s: index(s, i))
+
+    for d in range(D):
+        wait_bytes(part_recv[1][d].at[pl.ds(0, (mid - 1) * A)], s_recv.at[2 * D + d])
+
+
+    def send_far(y, h):
+        @pl.when(jnp.logical_not(late))
+        def _():
+            far_copy(y, h).start()
+
+    stage(0, gather_part(1), send_far, groups)
+    for c in range(D):
         wait_bytes(recv[c].at[pl.ds(0, (S - 1) * A)], s_recv.at[c])
-        stage(c, gather_full(c), lambda y, h: fac_copy(c, y, h), groups - H)
+    stage(1, lambda i: gather(recv, lambda s: aidx[s, fac, i]), lambda y, h: fac_copy(1, y, h).start(), groups - H)
+
+    @pl.when(late)
+    def _():
+        def one(g, _):
+            far_copy(g // H, g % H).start()
+            return 0
+
+        lax.fori_loop(0, groups, one, 0)
+
+    for d in range(D):
+        wait_bytes(part_recv[0][d].at[pl.ds(0, (mid - 1) * A)], s_recv.at[D + d])
+    stage(2, gather_part(0), lambda y, h: fac_copy(2, y, h).start(), groups - H)
 
     wait_bytes(half_send, s_send)
     wait_bytes(pair_recv, p_send)
     for n in range(2):
-        wait_bytes(pair_recv.at[pl.ds(0, C), pl.ds(0, chips - 1)], f_sem.at[n])
+        wait_bytes(pair_recv.at[pl.ds(0, 2), pl.ds(0, chips - 1)], f_sem.at[n])
         wait_bytes(pair_recv.at[0], x_sem.at[n])
 
 
-def finish_kernel(T, rows, terms, far, out, wide, sem):
+def finish_kernel(rows, terms, far, out, wide, sem):
     slots, parts, per, width = terms.shape
     count = per // rows
+    kept = width - far.shape[3]
 
     def copy(p, r):
         block = pl.ds(pl.multiple_of(r * rows, rows), rows)
@@ -641,8 +668,8 @@
             block = pl.ds(pl.multiple_of(r * rows, rows), rows)
             value = sum(terms[n, p, block, :].astype(jnp.float32) for n in range(slots))
             tail = sum(far[n, p, block, :].astype(jnp.float32) for n in range(slots))
-            wide[p, block, : width - T] = value[:, : width - T]
-            wide[p, block, width - T :] = value[:, width - T :] + tail
+            wide[p, block, : kept] = value[:, : kept]
+            wide[p, block, kept :] = value[:, kept :] + tail
             copy(p, r).start()
             return 0
 
@@ -665,7 +692,9 @@
     A = height // T
     C = width // S // T
     mid = S // 2
-    assert F == 2 * NF and parts == 2 and NF % 2 == 0 and height % T == 0 and S % 2 == 0
+    D = C // 2
+    assert C % 2 == 0
+    assert F == 2 * NF and parts == 2 and NF % 2 == 0 and height % T == 0 and S % 4 == 0
     per = total // F
     H = math.gcd(per // T, 4)
     ids = (beta_index.transpose(2, 0, 1), alpha_index.transpose(2, 0, 1), beta_tile, alpha_tile)
@@ -677,15 +706,15 @@
         functools.partial(halves_kernel, (S, F, C, A, T, K, NB, H)),
         out_shape=(
             pltpu.VMEM((NF // 2, parts, per, width // S), bf16),
-            pltpu.VMEM((NF // 2, parts, per, T), bf16),
+            pltpu.VMEM((NF // 2, parts, per, D * T), bf16),
         ),
         in_specs=[hbm] * 9,
         out_specs=(vmem, vmem),
         scratch_shapes=[
             pltpu.VMEM((NB, height, T), bf16),
-            pltpu.VMEM(((C - 1) * (S - 1) + 2 * (mid - 1), A, T, T), bf16),
-            pltpu.VMEM((C + 1, total, T), bf16),
-            pltpu.VMEM((C + 1, F // 2, H, per // H, T), bf16),
+            pltpu.VMEM((D * (S - 1) + 2 * D * (mid - 1), A, T, T), bf16),
+            pltpu.VMEM((3, total, D * T), bf16),
+            pltpu.VMEM((3, F // 2, H, per // H, D * T), bf16),
             pltpu.VMEM((K * T, T), bf16),
             pltpu.VMEM((T, K * T), bf16),
             pltpu.VMEM((NF, width), jnp.int32),
@@ -700,15 +729,15 @@
             pltpu.SMEM((NF, K), jnp.int32),
             pltpu.VMEM((height, width), bf16),
         ]
-        + [pltpu.VMEM((NB, T, T), bf16) for _ in range(C - 1)]
-        + [pltpu.VMEM((mid * A + 1, T, T), bf16) for _ in range(2)]
-        + [dma((A,)), dma((8,)), dma, dma((C + 1,)), dma, dma((2, F // 2, H)), dma((2,)), dma((2,))],
+        + [pltpu.VMEM((NB, T, T), bf16) for _ in range(D)]
+        + [pltpu.VMEM((mid * A + 1, T, T), bf16) for _ in range(2 * D)]
+        + [dma((A,)), dma((8,)), dma, dma((3 * D,)), dma, dma((2, F // 2, H)), dma((2,)), dma((2,))],
         compiler_params=pltpu.CompilerParams(collective_id=0, has_side_effects=True, vmem_limit_bytes=48 << 20),
         name="sigma",
     )(*[pltpu.with_memory_space_constraint(x, pltpu.HBM) for x in (amplitudes, beta_flip, alpha_flip, beta_tiles, alpha_tiles, *ids)])
     rows = math.gcd(per, 128)
     return pl.pallas_call(
-        functools.partial(finish_kernel, T, rows),
+        functools.partial(finish_kernel, rows),
         out_shape=jax.ShapeDtypeStruct((parts, per, width // S), jnp.float32),
         in_specs=[vmem, vmem],
         out_specs=pl.BlockSpec(memory_space=pltpu.HBM),
@@ -720,7 +749,7 @@
 
 def either(S, F, *args):
     height, width, T = args[0].shape[1], args[0].shape[2], args[7].shape[1]
-    form = halves if width // S >= 2 * T and height % T == 0 and S % 2 == 0 else local
+    form = halves if width // S % (2 * T) == 0 and height % T == 0 and S % 4 == 0 else local
     return form(S, F, *args)
 
 

time: 102 us -> 97.2 us (0.953)
  the two profiles are of different devices: /device:TPU:0 before, /device:TPU:12 now
where the time goes in v3:
time: 97.2 us; the launch traced here: 97 us
  Pallas kernels  97 us (100%)
    pallas_call x1, Pallas kernels, halves(): pl.pallas_call(functools.partial(halves_kernel, (S, F, C, A, T, K, NB, H)...  94.9 us
    pallas_call x1, Pallas kernels, halves(): pl.pallas_call(functools.partial(finish_kernel, rows), out_shape=jax.Shap...  2.15 us

profile of v3, /device:TPU:12, one launch (start us, length us, event | category | flops | bytes accessed | tf_op | source)
XLA Modules:
  0.0 97.0 jit_solution(9425300206639352286)
XLA Ops:
  0.0 94.9 %sigma.1 = (bf16[1,2,1024,512]{3,2,1,0:T(8,128)(2,1)S(1)}, bf16[1,2,1024,256]{3,2,1,0:T(8,128)(2,1)S(1)}) custom-call(bf16[2,512,4096]{2,1,0:T(8,128)(2,1)} %amp_hbm.1, s32[2,4096]{1,0:T(2,128)} %bflip_hbm.1, s32[2,4096]{1,0:T(2,128)} %aflip_hbm.1, bf16[16,128,128]{2,1,0:T(8,128)(2,1)} %btab_hbm.1, bf16[16,128,128]{2,1,0:T(8,128)(2,1)} %atab_hbm.1, ...), custom_call_target="tpu_custom_call" | custom-call | tf_op jit(solution)/shard_map/sigma/pallas_call | solution.py:705
  94.9 2.2 %finish.1 = f32[2,1024,512]{2,1,0:T(8,128)} custom-call(bf16[1,2,1024,512]{3,2,1,0:T(8,128)(2,1)S(1)} %get-tuple-element.7.terms, bf16[1,2,1024,256]{3,2,1,0:T(8,128)(2,1)S(1)} %get-tuple-element.8.far), custom_call_target="tpu_custom_call" | custom-call | tf_op jit(solution)/shard_map/finish/pallas_call | solution.py:739

commit v4 on v3

--- a/solution.py
+++ b/solution.py
@@ -332,7 +332,7 @@
 
 
     def far(t):
-        at = swap(me, t, t // 2) if mid == 4 else (me + t) % mid
+        at = swap(me, t + 1, t // 2) if mid == 4 else (me + t) % mid
         return (1 - side) * mid + at
 
     def near(t):
@@ -376,10 +376,7 @@
 
     for copy in tables[:5]:
         copy.start()
-    for a in range(A):
-        load(a).start()
-    for copy in tables[5:]:
-        copy.start()
+    load(0).start()
 
     def signs(flips, start, size):
         value = flips[:, pl.ds(start, size)]
@@ -444,7 +441,6 @@
         )
 
     def sign(a):
-        load(a).wait()
         rows = pl.ds(pl.multiple_of(a * T, T), T)
         row_sign = sign_a[rows, :]
         for k in range(NB):
@@ -462,12 +458,18 @@
         for t in range(mid):
             strip_copy(far(t), a).start()
 
+    load(0).wait()
+    for a in range(1, A):
+        load(a).start()
+    for copy in tables[5:]:
+        copy.start()
     sign(0)
     strip(0)
     pl.semaphore_wait(barrier, S - 1 + 2 * chips - 1)
     send_strip(0)
 
     def each_strip(a, _):
+        load(a).wait()
         sign(a)
         strip(a)
         send_strip(a)
@@ -660,7 +662,7 @@
 
     def copy(p, r):
         block = pl.ds(pl.multiple_of(r * rows, rows), rows)
-        return pltpu.make_async_copy(wide.at[p, block], out.at[p, block], sem.at[p, r])
+        return pltpu.make_async_copy(wide.at[p, block], out.at[p, block], sem)
 
     for p in range(parts):
 
@@ -675,13 +677,7 @@
 
         lax.fori_loop(0, count, convert, 0)
 
-    for p in range(parts):
-
-        def wait(r, _):
-            copy(p, r).wait()
-            return 0
-
-        lax.fori_loop(0, count, wait, 0)
+    pltpu.make_async_copy(wide, out, sem).wait()
 
 
 def halves(S, F, amplitudes, beta_index, beta_tile, beta_flip, alpha_index, alpha_tile, alpha_flip, beta_tiles, alpha_tiles):
@@ -741,7 +737,7 @@
         out_shape=jax.ShapeDtypeStruct((parts, per, width // S), jnp.float32),
         in_specs=[vmem, vmem],
         out_specs=pl.BlockSpec(memory_space=pltpu.HBM),
-        scratch_shapes=[pltpu.VMEM((parts, per, width // S), jnp.float32), dma((parts, per // rows))],
+        scratch_shapes=[pltpu.VMEM((parts, per, width // S), jnp.float32), dma],
         compiler_params=pltpu.CompilerParams(vmem_limit_bytes=16 << 20),
         name="finish",
     )(terms, far)

time: 97.2 us -> 96.9 us (level)
  the two profiles are of different devices: /device:TPU:12 before, /device:TPU:0 now
where the time goes in v4:
time: 96.9 us; the launch traced here: 95.4 us
  Pallas kernels  95.4 us (98%)
    pallas_call x1, Pallas kernels, halves(): pl.pallas_call(functools.partial(halves_kernel, (S, F, C, A, T, K, NB, H)...  93.4 us
    pallas_call x1, Pallas kernels, halves(): pl.pallas_call(functools.partial(finish_kernel, rows), out_shape=jax.Shap...  2.02 us

profile of v4, /device:TPU:0, one launch (start us, length us, event | category | flops | bytes accessed | tf_op | source)
XLA Modules:
  0.0 95.4 jit_solution(6290975637329856531)
XLA Ops:
  0.0 93.4 %sigma.1 = (bf16[1,2,1024,512]{3,2,1,0:T(8,128)(2,1)S(1)}, bf16[1,2,1024,256]{3,2,1,0:T(8,128)(2,1)S(1)}) custom-call(bf16[2,512,4096]{2,1,0:T(8,128)(2,1)} %amp_hbm.1, s32[2,4096]{1,0:T(2,128)} %bflip_hbm.1, s32[2,4096]{1,0:T(2,128)} %aflip_hbm.1, bf16[16,128,128]{2,1,0:T(8,128)(2,1)} %btab_hbm.1, bf16[16,128,128]{2,1,0:T(8,128)(2,1)} %atab_hbm.1, ...), custom_call_target="tpu_custom_call" | custom-call | tf_op jit(solution)/shard_map/sigma/pallas_call | solution.py:701
  93.4 2.0 %finish.1 = f32[2,1024,512]{2,1,0:T(8,128)} custom-call(bf16[1,2,1024,512]{3,2,1,0:T(8,128)(2,1)S(1)} %get-tuple-element.7.terms, bf16[1,2,1024,256]{3,2,1,0:T(8,128)(2,1)S(1)} %get-tuple-element.8.far), custom_call_target="tpu_custom_call" | custom-call | tf_op jit(solution)/shard_map/finish/pallas_call | solution.py:735

commit v5 on v4

--- a/solution.py
+++ b/solution.py
@@ -342,7 +342,7 @@
     barrier = pltpu.get_barrier_semaphore()
 
     def greet_str(t, _):
-        pl.semaphore_signal(barrier, inc=1, device_id={"str": (me + 1 + t) % S}, device_id_type=MESH)
+        pl.semaphore_signal(barrier, inc=1, device_id={"str": (me + 1 + (t + mid - 1) % (S - 1)) % S}, device_id_type=MESH)
         return 0
 
     def greet_fac(t, _):
@@ -371,12 +371,13 @@
         )
     ]
 
-    def load(a):
-        return pltpu.make_async_copy(amp_hbm.at[part, pl.ds(a * T, T)], raw.at[pl.ds(a * T, T)], a_sem.at[a])
+    def load(a, n):
+        rows = pl.ds(a * T, n * T)
+        return pltpu.make_async_copy(amp_hbm.at[part, rows], raw.at[rows], a_sem.at[a])
 
     for copy in tables[:5]:
         copy.start()
-    load(0).start()
+    load(0, 1).start()
 
     def signs(flips, start, size):
         value = flips[:, pl.ds(start, size)]
@@ -458,9 +459,8 @@
         for t in range(mid):
             strip_copy(far(t), a).start()
 
-    load(0).wait()
-    for a in range(1, A):
-        load(a).start()
+    load(0, 1).wait()
+    load(1, A - 1).start()
     for copy in tables[5:]:
         copy.start()
     sign(0)
@@ -469,12 +469,12 @@
     send_strip(0)
 
     def each_strip(a, _):
-        load(a).wait()
         sign(a)
         strip(a)
         send_strip(a)
         return 0
 
+    load(1, A - 1).wait()
     lax.fori_loop(1, A, each_strip, 0)
 
     def beta(j):
@@ -692,7 +692,7 @@
     assert C % 2 == 0
     assert F == 2 * NF and parts == 2 and NF % 2 == 0 and height % T == 0 and S % 4 == 0
     per = total // F
-    H = math.gcd(per // T, 4)
+    H = math.gcd(per // T, 2)
     ids = (beta_index.transpose(2, 0, 1), alpha_index.transpose(2, 0, 1), beta_tile, alpha_tile)
     hbm = pl.BlockSpec(memory_space=pltpu.HBM)
     vmem = pl.BlockSpec(memory_space=pltpu.VMEM)
@@ -727,7 +727,7 @@
         ]
         + [pltpu.VMEM((NB, T, T), bf16) for _ in range(D)]
         + [pltpu.VMEM((mid * A + 1, T, T), bf16) for _ in range(2 * D)]
-        + [dma((A,)), dma((8,)), dma, dma((3 * D,)), dma, dma((2, F // 2, H)), dma((2,)), dma((2,))],
+        + [dma((2,)), dma((8,)), dma, dma((3 * D,)), dma, dma((2, F // 2, H)), dma((2,)), dma((2,))],
         compiler_params=pltpu.CompilerParams(collective_id=0, has_side_effects=True, vmem_limit_bytes=48 << 20),
         name="sigma",
     )(*[pltpu.with_memory_space_constraint(x, pltpu.HBM) for x in (amplitudes, beta_flip, alpha_flip, beta_tiles, alpha_tiles, *ids)])
@@ -745,7 +745,7 @@
 
 def either(S, F, *args):
     height, width, T = args[0].shape[1], args[0].shape[2], args[7].shape[1]
-    form = halves if width // S % (2 * T) == 0 and height % T == 0 and S % 4 == 0 else local
+    form = halves if width // S % (2 * T) == 0 and height >= 2 * T and height % T == 0 and S % 4 == 0 else local
     return form(S, F, *args)
 
 

time: 96.9 us -> 97.2 us (level); the launches traced: 95.4 us -> 97.1 us
  Pallas kernels: 95.4 us -> 97.1 us
    pallas_call x1, Pallas kernels: 93.4 us -> 95.1 us  [halves(): pl.pallas_call(functools.partial(halves_kernel, (S, F, C, A, T, K, NB, H)...]
where the time goes in v5:
time: 97.2 us; the launch traced here: 97.1 us
  Pallas kernels  97.1 us (100%)
    pallas_call x1, Pallas kernels, halves(): pl.pallas_call(functools.partial(halves_kernel, (S, F, C, A, T, K, NB, H)...  95.1 us
    pallas_call x1, Pallas kernels, halves(): pl.pallas_call(functools.partial(finish_kernel, rows), out_shape=jax.Shap...  2.02 us

profile of v5, /device:TPU:0, one launch (start us, length us, event | category | flops | bytes accessed | tf_op | source)
XLA Modules:
  0.0 97.1 jit_solution(14546388909122822680)
XLA Ops:
  0.0 95.1 %sigma.1 = (bf16[1,2,1024,512]{3,2,1,0:T(8,128)(2,1)S(1)}, bf16[1,2,1024,256]{3,2,1,0:T(8,128)(2,1)S(1)}) custom-call(bf16[2,512,4096]{2,1,0:T(8,128)(2,1)} %amp_hbm.1, s32[2,4096]{1,0:T(2,128)} %bflip_hbm.1, s32[2,4096]{1,0:T(2,128)} %aflip_hbm.1, bf16[16,128,128]{2,1,0:T(8,128)(2,1)} %btab_hbm.1, bf16[16,128,128]{2,1,0:T(8,128)(2,1)} %atab_hbm.1, ...), custom_call_target="tpu_custom_call" | custom-call | tf_op jit(solution)/shard_map/sigma/pallas_call | solution.py:701
  95.1 2.0 %finish.1 = f32[2,1024,512]{2,1,0:T(8,128)} custom-call(bf16[1,2,1024,512]{3,2,1,0:T(8,128)(2,1)S(1)} %get-tuple-element.7.terms, bf16[1,2,1024,256]{3,2,1,0:T(8,128)(2,1)S(1)} %get-tuple-element.8.far), custom_call_target="tpu_custom_call" | custom-call | tf_op jit(solution)/shard_map/finish/pallas_call | solution.py:735
